TPU v7x, 32 devices: a whole 2x2x4 slice. The times are simulated.
32 devices in a mesh: blk: 8 (over z, y), uly: 4 (over x, core).
Axes of the slice: x: 2, y: 2, z: 4, core: 2. Of those that a mesh axis runs over, the one named last changes fastest.
Arguments:
- tokens: bfloat16 [6400, 1024], P(('blk', 'uly')), may hold values from -6 to 6
- cotangent: bfloat16 [6400, 1024], P(('blk', 'uly')), may hold values from -6 to 6
- noise_embed: bfloat16 [64, 1024], P(('blk', 'uly')), may hold values from -6 to 6
- frame_clip: int32 [64], replicated, may hold values from 0 to 8, as said below
- frame_index: int32 [64], replicated, may hold values from 0 to 31, as said below
- mod_weight: bfloat16 [1024, 6144], replicated, may hold values from -0.1875 to 0.1875
- mod_bias: bfloat16 [6144], replicated, may hold values from -3 to 3
- attn_weight: bfloat16 [1024, 3072], replicated, may hold values from -0.1875 to 0.1875
- attn_bias: bfloat16 [3072], replicated, may hold values from -3 to 3
- proj_weight: bfloat16 [1024, 1024], replicated, may hold values from -3 to 3
- proj_bias: bfloat16 [1024], replicated, may hold values from -3 to 3
- up_weight: bfloat16 [1024, 4096], replicated, may hold values from -0.1875 to 0.1875
- up_bias: bfloat16 [4096], replicated, may hold values from -3 to 3
- down_weight: bfloat16 [4096, 1024], replicated, may hold values from -0.09375 to 0.09375
- down_bias: bfloat16 [1024], replicated, may hold values from -3 to 3
Outputs:
- output: bfloat16 [6400, 1024], P(('blk', 'uly'))
- token_grad: float32 [6400, 1024], P(('blk', 'uly'))
- grad_mod_weight: float32 [1024, 6144], P(('blk', 'uly'))
- grad_mod_bias: float32 [6144], P(('blk', 'uly'))
- grad_attn_weight: float32 [1024, 3072], P(('blk', 'uly'))
- grad_attn_bias: float32 [3072], P(('blk', 'uly'))
- grad_proj_weight: float32 [1024, 1024], P(('blk', 'uly'))
- grad_proj_bias: float32 [1024], P(('blk', 'uly'))
- grad_up_weight: float32 [1024, 4096], P(('blk', 'uly'))
- grad_up_bias: float32 [4096], P(('blk', 'uly'))
- grad_down_weight: float32 [4096, 1024], P(('blk', 'uly'))
- grad_down_bias: float32 [1024], P(('blk', 'uly'))
Inputs may be any that keep to these rules, and one draw needn't show every extreme that they name: `frame_clip`: block b holds frames b * 8 to (b + 1) * 8 - 1. Of these, 4 consecutive frames, either the first or the last ones of the block, form one short clip with id b, and the other 4 frames belong to the one long clip, whose id is the number of blocks and which has frames in every block, 32 in all. `frame_index`: the frame's place within its clip, counting from 0 at the clip's first frame; the long clip's places rise with the frame number.
All inputs are finite; a program needn't handle non-finite values.
Results may differ from a plain program's by a relative error of at most 0.015.
The roundings to bfloat16 on the way count: a program that leaves them out, or rounds other values in their place, can miss the bound.
Values may be sent and summed in bfloat16 or wider, within the bound.
No kernel may reach another device: no remote copies, remote signals or barrier semaphores. Data moves between devices by JAX's collectives and lax.ppermute only.
A program may use at most 320 MiB of HBM per device.

v0:
```python
import math
import jax
import jax.numpy as jnp
from jax import lax
from jax.sharding import PartitionSpec as P

DH = 64
GRID = 10
FB = 8
PATCH = 100
GELU_C = 0.7978845608028654
GELU_K = 0.044715
NEG_BIG = -1e30


def layer_norm(values):
    center = values - jnp.mean(values, axis=-1, keepdims=True)
    inv_std = lax.rsqrt(jnp.mean(center * center, axis=-1, keepdims=True) + 1e-06)
    return (center * inv_std, inv_std)


def norm_back(grad, normed, inv_std):
    return inv_std * (
        grad
        - jnp.mean(grad, axis=-1, keepdims=True)
        - normed * jnp.mean(grad * normed, axis=-1, keepdims=True)
    )


def rope_table(time_pos, row_pos, col_pos):
    half = DH // 2
    n_time = DH // 8
    n_row = 3 * DH // 16
    pair = jnp.arange(half, dtype=jnp.int32)
    in_time = pair < n_time
    in_row = (pair >= n_time) & (pair < n_time + n_row)
    local = jnp.where(in_time, pair, jnp.where(in_row, pair - n_time, pair - n_time - n_row))
    total = jnp.where(in_time, n_time, n_row)
    frequency = jnp.exp(-math.log(10000.0) * local.astype(jnp.float32) / total.astype(jnp.float32))
    place = jnp.where(
        in_time[None, :],
        time_pos[:, None],
        jnp.where(in_row[None, :], row_pos[:, None], col_pos[:, None]),
    )
    angle = place.astype(jnp.float32) * frequency[None, :]
    return (jnp.cos(angle), jnp.sin(angle))


def rotate(values, cosine, sine, sign):
    rows = values.shape[0]
    pairs = values.reshape(rows, -1, DH // 2, 2)
    first = pairs[..., 0]
    second = pairs[..., 1]
    cos_part = cosine[:, None, :]
    sin_part = sign * sine[:, None, :]
    turned = jnp.stack(
        [first * cos_part - second * sin_part, first * sin_part + second * cos_part], axis=-1
    )
    return turned.reshape(values.shape)


def on_device(
    tokens,
    cotangent,
    noise_embed,
    frame_clip,
    frame_index,
    mod_weight,
    mod_bias,
    attn_weight,
    attn_bias,
    proj_weight,
    proj_bias,
    up_weight,
    up_bias,
    down_weight,
    down_bias,
):
    n_uly = lax.axis_size("uly")
    n_blk = lax.axis_size("blk")
    blk_index = lax.axis_index("blk")
    uly_index = lax.axis_index("uly")
    tok_dev, width = tokens.shape
    frames_dev = noise_embed.shape[0]
    block_tok = tok_dev * n_uly
    head_cols = width // n_uly
    heads_dev = head_cols // DH
    scale = 1.0 / math.sqrt(DH)
    patch = jnp.arange(PATCH, dtype=jnp.int32)
    row_of = patch // GRID
    col_of = patch % GRID
    block_clip = lax.dynamic_slice_in_dim(frame_clip, blk_index * FB, FB)
    block_time = lax.dynamic_slice_in_dim(frame_index, blk_index * FB, FB)
    own_time = lax.dynamic_slice_in_dim(block_time, uly_index * frames_dev, frames_dev)
    cos_own, sin_own = rope_table(
        jnp.repeat(own_time, PATCH), jnp.tile(row_of, frames_dev), jnp.tile(col_of, frames_dev)
    )
    cos_blk, sin_blk = rope_table(
        jnp.repeat(block_time, PATCH), jnp.tile(row_of, FB), jnp.tile(col_of, FB)
    )
    silu_noise = jax.nn.silu(noise_embed.astype(jnp.float32)).astype(jnp.bfloat16)
    mod = jnp.dot(silu_noise, mod_weight, preferred_element_type=jnp.float32) + mod_bias.astype(
        jnp.float32
    )
    shift1, scale1, gate1, shift2, scale2, gate2 = [
        mod[:, None, j * width : (j + 1) * width] for j in range(6)
    ]
    framed = tokens.astype(jnp.float32).reshape(frames_dev, PATCH, width)
    normed1, inv_std1 = layer_norm(framed)
    hidden1 = (normed1 * (1.0 + scale1) + shift1).astype(jnp.bfloat16).reshape(tok_dev, width)
    qkv = jnp.dot(hidden1, attn_weight, preferred_element_type=jnp.float32) + attn_bias.astype(
        jnp.float32
    )
    q_tok = rotate(qkv[:, :width], cos_own, sin_own, 1.0).astype(jnp.bfloat16)
    k_tok = rotate(qkv[:, width : 2 * width], cos_own, sin_own, 1.0).astype(jnp.bfloat16)
    v_tok = qkv[:, 2 * width :].astype(jnp.bfloat16)
    q_heads, k_heads, v_heads = (
        lax.all_to_all(q_tok, "uly", split_axis=1, concat_axis=0, tiled=True),
        lax.all_to_all(k_tok, "uly", split_axis=1, concat_axis=0, tiled=True),
        lax.all_to_all(v_tok, "uly", split_axis=1, concat_axis=0, tiled=True),
    )
    k_every, v_every = (
        lax.all_gather(k_heads, "blk", axis=0, tiled=True),
        lax.all_gather(v_heads, "blk", axis=0, tiled=True),
    )
    group = 2
    n_pieces = n_blk // group
    piece_rows = group * block_tok
    key_pieces = k_every.reshape(n_pieces, piece_rows, heads_dev, DH)
    value_pieces = v_every.reshape(n_pieces, piece_rows, heads_dev, DH)
    clip_pieces = jnp.repeat(frame_clip, PATCH).reshape(n_pieces, piece_rows)
    time_pieces = jnp.repeat(frame_index, PATCH).reshape(n_pieces, piece_rows)
    query_clip = jnp.repeat(block_clip, PATCH)
    query_time = jnp.repeat(block_time, PATCH)
    queries = q_heads.reshape(block_tok, heads_dev, DH)

    def piece_score(k_rows, clip_k, time_k):
        allowed = (query_clip[:, None] == clip_k[None, :]) & (
            time_k[None, :] <= query_time[:, None]
        )
        score = (
            jnp.einsum("qhd,khd->hqk", queries, k_rows, preferred_element_type=jnp.float32) * scale
        )
        return (allowed, jnp.where(allowed[None], score, NEG_BIG))

    def gather_stats(carry, pieces):
        top, total = carry
        k_rows, clip_k, time_k = pieces
        allowed, score = piece_score(k_rows, clip_k, time_k)
        new_top = jnp.maximum(top, jnp.max(score, axis=-1))
        expo = jnp.where(allowed[None], jnp.exp(score - new_top[..., None]), 0.0)
        total = total * jnp.exp(top - new_top) + jnp.sum(expo, axis=-1)
        return ((new_top, total), None)

    start_top = jnp.full((heads_dev, block_tok), NEG_BIG, jnp.float32)
    start_total = jnp.zeros((heads_dev, block_tok), jnp.float32)
    (top_all, total_all), _ = lax.scan(
        gather_stats, (start_top, start_total), (key_pieces, clip_pieces, time_pieces)
    )
    log_total = top_all + jnp.log(total_all)

    def mix_values(carry, pieces):
        acc_low, acc_exact = carry
        k_rows, v_rows, clip_k, time_k = pieces
        allowed, score = piece_score(k_rows, clip_k, time_k)
        prob = jnp.where(allowed[None], jnp.exp(score - log_total[..., None]), 0.0)
        acc_low = acc_low + jnp.einsum(
            "hqk,khd->qhd", prob.astype(jnp.bfloat16), v_rows, preferred_element_type=jnp.float32
        )
        acc_exact = acc_exact + jnp.einsum(
            "hqk,khd->qhd", prob, v_rows.astype(jnp.float32), preferred_element_type=jnp.float32
        )
        return ((acc_low, acc_exact), None)

    zero_rows = jnp.zeros((block_tok, heads_dev, DH), jnp.float32)
    (mixed_low, mixed_exact), _ = lax.scan(
        mix_values, (zero_rows, zero_rows), (key_pieces, value_pieces, clip_pieces, time_pieces)
    )
    attn_heads = mixed_low.reshape(block_tok, head_cols).astype(jnp.bfloat16)
    attn_tok = lax.all_to_all(attn_heads, "uly", split_axis=0, concat_axis=1, tiled=True)
    branch = (
        jnp.dot(attn_tok, proj_weight, preferred_element_type=jnp.float32)
        + proj_bias.astype(jnp.float32)
    ).reshape(frames_dev, PATCH, width)
    resid = framed + gate1 * branch
    normed2, inv_std2 = layer_norm(resid)
    hidden2 = (normed2 * (1.0 + scale2) + shift2).astype(jnp.bfloat16).reshape(tok_dev, width)
    pre = jnp.dot(hidden2, up_weight, preferred_element_type=jnp.float32) + up_bias.astype(
        jnp.float32
    )
    inner_tanh = jnp.tanh(GELU_C * (pre + GELU_K * pre * pre * pre))
    act = (0.5 * pre * (1.0 + inner_tanh)).astype(jnp.bfloat16)
    mlp = (
        jnp.dot(act, down_weight, preferred_element_type=jnp.float32)
        + down_bias.astype(jnp.float32)
    ).reshape(frames_dev, PATCH, width)
    output = (resid + gate2 * mlp).reshape(tok_dev, width).astype(jnp.bfloat16)
    dy_grad = cotangent.astype(jnp.float32).reshape(frames_dev, PATCH, width)
    gate2_grad = jnp.sum(dy_grad * mlp, axis=1)
    mlp_grad = (gate2 * dy_grad).astype(jnp.bfloat16).reshape(tok_dev, width)
    g_down_weight = jnp.einsum("tf,td->fd", act, mlp_grad, preferred_element_type=jnp.float32)
    g_down_bias = jnp.sum(mlp_grad.astype(jnp.float32), axis=0)
    act_grad = jnp.einsum("td,fd->tf", mlp_grad, down_weight, preferred_element_type=jnp.float32)
    slope = 0.5 * (1.0 + inner_tanh) + 0.5 * pre * (1.0 - inner_tanh * inner_tanh) * GELU_C * (
        1.0 + 3.0 * GELU_K * pre * pre
    )
    pre_grad = (act_grad * slope).astype(jnp.bfloat16)
    g_up_weight = jnp.einsum("td,tf->df", hidden2, pre_grad, preferred_element_type=jnp.float32)
    g_up_bias = jnp.sum(pre_grad.astype(jnp.float32), axis=0)
    hid2_grad = jnp.einsum(
        "tf,df->td", pre_grad, up_weight, preferred_element_type=jnp.float32
    ).reshape(frames_dev, PATCH, width)
    shift2_grad = jnp.sum(hid2_grad, axis=1)
    scale2_grad = jnp.sum(hid2_grad * normed2, axis=1)
    resid_grad = dy_grad + norm_back(hid2_grad * (1.0 + scale2), normed2, inv_std2)
    gate1_grad = jnp.sum(resid_grad * branch, axis=1)
    branch_grad = (gate1 * resid_grad).astype(jnp.bfloat16).reshape(tok_dev, width)
    g_proj_weight = jnp.einsum(
        "td,te->de", attn_tok, branch_grad, preferred_element_type=jnp.float32
    )
    g_proj_bias = jnp.sum(branch_grad.astype(jnp.float32), axis=0)
    attn_grad_tok = jnp.einsum(
        "te,de->td", branch_grad, proj_weight, preferred_element_type=jnp.float32
    ).astype(jnp.bfloat16)
    attn_grad = lax.all_to_all(
        attn_grad_tok, "uly", split_axis=1, concat_axis=0, tiled=True
    ).reshape(block_tok, heads_dev, DH)
    row_delta = jnp.einsum("qhd,qhd->hq", attn_grad.astype(jnp.float32), mixed_exact)

    def back_piece(query_acc, pieces):
        k_rows, v_rows, clip_k, time_k = pieces
        allowed, score = piece_score(k_rows, clip_k, time_k)
        prob = jnp.where(allowed[None], jnp.exp(score - log_total[..., None]), 0.0)
        prob_grad = jnp.einsum(
            "qhd,khd->hqk", attn_grad, v_rows, preferred_element_type=jnp.float32
        )
        score_grad = (prob * (prob_grad - row_delta[..., None])).astype(jnp.bfloat16)
        query_acc = (
            query_acc
            + jnp.einsum("hqk,khd->qhd", score_grad, k_rows, preferred_element_type=jnp.float32)
            * scale
        )
        key_rows = (
            jnp.einsum("hqk,qhd->khd", score_grad, queries, preferred_element_type=jnp.float32)
            * scale
        )
        value_rows = jnp.einsum(
            "hqk,qhd->khd", prob.astype(jnp.bfloat16), attn_grad, preferred_element_type=jnp.float32
        )
        return (query_acc, (key_rows, value_rows))

    query_grad, (key_terms, value_terms) = lax.scan(
        back_piece, zero_rows, (key_pieces, value_pieces, clip_pieces, time_pieces)
    )
    key_terms = key_terms.reshape(n_blk * block_tok, head_cols)
    value_terms = value_terms.reshape(n_blk * block_tok, head_cols)
    key_local, value_local = (
        lax.psum_scatter(
            key_terms.astype(jnp.bfloat16), "blk", scatter_dimension=0, tiled=True
        ).astype(jnp.float32),
        lax.psum_scatter(
            value_terms.astype(jnp.bfloat16), "blk", scatter_dimension=0, tiled=True
        ).astype(jnp.float32),
    )
    dq_heads = rotate(query_grad.reshape(block_tok, head_cols), cos_blk, sin_blk, -1.0).astype(
        jnp.bfloat16
    )
    dk_heads = rotate(key_local, cos_blk, sin_blk, -1.0).astype(jnp.bfloat16)
    dv_heads = value_local.astype(jnp.bfloat16)
    dq_tok, dk_tok, dv_tok = (
        lax.all_to_all(dq_heads, "uly", split_axis=0, concat_axis=1, tiled=True),
        lax.all_to_all(dk_heads, "uly", split_axis=0, concat_axis=1, tiled=True),
        lax.all_to_all(dv_heads, "uly", split_axis=0, concat_axis=1, tiled=True),
    )
    qkv_grad = jnp.concatenate([dq_tok, dk_tok, dv_tok], axis=1)
    g_attn_weight = jnp.einsum("td,te->de", hidden1, qkv_grad, preferred_element_type=jnp.float32)
    g_attn_bias = jnp.sum(qkv_grad.astype(jnp.float32), axis=0)
    hid1_grad = jnp.einsum(
        "te,de->td", qkv_grad, attn_weight, preferred_element_type=jnp.float32
    ).reshape(frames_dev, PATCH, width)
    shift1_grad = jnp.sum(hid1_grad, axis=1)
    scale1_grad = jnp.sum(hid1_grad * normed1, axis=1)
    token_grad = (resid_grad + norm_back(hid1_grad * (1.0 + scale1), normed1, inv_std1)).reshape(
        tok_dev, width
    )
    mod_grad = jnp.concatenate(
        [shift1_grad, scale1_grad, gate1_grad, shift2_grad, scale2_grad, gate2_grad], axis=1
    )
    g_mod_weight = jnp.einsum(
        "fd,fe->de",
        silu_noise.astype(jnp.float32),
        mod_grad,
        precision=lax.Precision.HIGHEST,
        preferred_element_type=jnp.float32,
    )
    g_mod_bias = jnp.sum(mod_grad, axis=0)
    (
        g_mod_weight,
        g_mod_bias,
        g_attn_weight,
        g_attn_bias,
        g_proj_weight,
        g_proj_bias,
        g_up_weight,
        g_up_bias,
        g_down_weight,
        g_down_bias,
    ) = (
        lax.psum_scatter(g_mod_weight, ("blk", "uly"), scatter_dimension=0, tiled=True),
        lax.psum_scatter(g_mod_bias, ("blk", "uly"), scatter_dimension=0, tiled=True),
        lax.psum_scatter(g_attn_weight, ("blk", "uly"), scatter_dimension=0, tiled=True),
        lax.psum_scatter(g_attn_bias, ("blk", "uly"), scatter_dimension=0, tiled=True),
        lax.psum_scatter(g_proj_weight, ("blk", "uly"), scatter_dimension=0, tiled=True),
        lax.psum_scatter(g_proj_bias, ("blk", "uly"), scatter_dimension=0, tiled=True),
        lax.psum_scatter(g_up_weight, ("blk", "uly"), scatter_dimension=0, tiled=True),
        lax.psum_scatter(g_up_bias, ("blk", "uly"), scatter_dimension=0, tiled=True),
        lax.psum_scatter(g_down_weight, ("blk", "uly"), scatter_dimension=0, tiled=True),
        lax.psum_scatter(g_down_bias, ("blk", "uly"), scatter_dimension=0, tiled=True),
    )
    return (
        output,
        token_grad,
        g_mod_weight,
        g_mod_bias,
        g_attn_weight,
        g_attn_bias,
        g_proj_weight,
        g_proj_bias,
        g_up_weight,
        g_up_bias,
        g_down_weight,
        g_down_bias,
    )


def solution(mesh):
    in_specs = (
        P(("blk", "uly"), None),
        P(("blk", "uly"), None),
        P(("blk", "uly"), None),
        P(),
        P(),
        P(),
        P(),
        P(),
        P(),
        P(),
        P(),
        P(),
        P(),
        P(),
        P(),
    )
    out_specs = (
        P(("blk", "uly"), None),
        P(("blk", "uly"), None),
        P(("blk", "uly"), None),
        P(("blk", "uly")),
        P(("blk", "uly"), None),
        P(("blk", "uly")),
        P(("blk", "uly"), None),
        P(("blk", "uly")),
        P(("blk", "uly"), None),
        P(("blk", "uly")),
        P(("blk", "uly"), None),
        P(("blk", "uly")),
    )
    return jax.shard_map(
        on_device, mesh=mesh, in_specs=in_specs, out_specs=out_specs, check_vma=False
    )
```

profile of v0, /device:TPU:0, one launch (start us, length us, event | category | flops | bytes accessed | tf_op | source)
XLA Modules:
  0.0 1709.3 jit_solution(14024680513358716793)
XLA Ops:
  44.5 11.9 all_to_all.131
  83.2 36.0 %all-gather.5.cloned.1.call-done = bf16[6400,256]{1,0:T(8,128)(2,1)} async-done(((bf16[800,256]{1,0:T(8,128)(2,1)}), bf16[6400,256]{1,0:T(8,128)(2,1)}) %all-gather.5.cloned.1.call-update) | async-done | bytes 3276816 | tf_op jit(solution)/shard_map/all_gather | solution.py:123
  119.3 10.4 reshape.865
  129.6 10.3 copy.84
  139.9 112.5 %while.41 = (s32[]{:T(128)}, f32[4,800]{1,0:T(4,128)S(1)}, f32[4,800]{1,0:T(4,128)}, s32[4,1600]{1,0:T(4,128)S(1)}, s32[4,1600]{1,0:T(4,128)S(1)}, /*index=5*/bf...) while((s32[]{:T(128)}, f32[4,800]{1,0:T(4,128)S(1)}, ...), condition=%wide.region_5.6_spmd.clone, body=%wide.region_2.5_spmd.clone.sunk | while | flops 700176000 | bytes 46394932 | solution.py:157
  144.0 13.0 fusion.152
  157.0 10.4 select_reduce_fusion.2
  172.3 12.9 fusion.152
  185.2 10.4 select_reduce_fusion.2
  200.4 12.9 fusion.152
  213.3 10.4 select_reduce_fusion.2
  228.4 12.9 fusion.152
  241.4 10.4 select_reduce_fusion.2
  252.4 10.4 reshape.864
  262.7 10.2 copy.83
  274.3 70.2 %while.42 = (s32[]{:T(128)}, f32[800,4,64]{0,2,1:T(8,128)}, f32[800,4,64]{0,2,1:T(8,128)S(1)}, bf16[4,1600,4,64]{1,3,2,0:T(8,128)(2,1)}, s32[4,1600]{1,0:T(4,128...) while((s32[]{:T(128)}, f32[800,4,64]{0,2,1:T(8,128)}, ...), condition=%wide.region_7.8_spmd.clone, body=%wide.region_6.7_spmd.clone.sunk | while | flops 1991219200 | bytes 60277552 | solution.py:176
  276.2 8.1 fusion.160
  293.7 8.1 fusion.160
  311.2 8.1 fusion.160
  384.5 9.4 convert_reduce_fusion
  414.3 184.9 %while.43 = (s32[]{:T(128)}, f32[800,4,64]{0,2,1:T(8,128)S(1)}, bf16[4,1600,4,64]{1,3,2,0:T(8,128)(2,1)}, bf16[4,1600,4,64]{1,3,2,0:T(8,128)(2,1)}, bf16[4,1600,...) while((s32[]{:T(128)}, f32[800,4,64]{0,2,1:T(8,128)S(1)}, ...), condition=%wide.region_13.14_spmd.clone, body=%wide.region_12.13_spmd.clone.sunk | while | flops 3322624000 | bytes 147058464 | solution.py:252
  416.2 11.7 fusion.173
  428.0 9.8 fusion.177
  437.7 12.5 fusion.174
  462.4 11.7 fusion.173
  474.2 9.7 fusion.177
  483.9 12.5 fusion.174
  508.6 11.7 fusion.173
  520.3 9.7 fusion.177
  530.0 12.5 fusion.174
  554.8 11.7 fusion.173
  566.5 9.7 fusion.177
  576.2 12.5 fusion.174
  599.2 10.5 copy.115
  609.7 10.6 reshape.862
  620.4 10.5 copy.114
  630.9 10.2 reshape.860
  646.5 48.1 %reduce-scatter.24.cloned.1.call-done = bf16[800,256]{1,0:T(8,128)(2,1)} async-done(((bf16[6400,256]{1,0:T(8,128)(2,1)}), bf16[800,256]{1,0:T(8,128)(2,1)}) %reduce-scatter.24.cloned.1.call-update) | async-done | bytes 409616 | tf_op jit(solution)/shard_map/reduce_scatter | solution.py:261
  698.0 75.6 %reduce-scatter.22.cloned.1.call-done = bf16[800,256]{1,0:T(8,128)(2,1)} async-done(((bf16[6400,256]{1,0:T(8,128)(2,1)}), bf16[800,256]{1,0:T(8,128)(2,1)}) %reduce-scatter.22.cloned.1.call-update) | async-done | bytes 409616
  797.6 9.7 all-to-all-done.5
  815.8 10.2 fusion.82
  827.5 8.2 fusion.89
  863.3 13.4 fusion.79
  877.5 41.1 %all-reduce.5 = (f32[6144]{0:T(1024)S(1)}, f32[3072]{0:T(1024)S(1)}, f32[1024]{0:T(1024)S(1)}, f32[4096]{0:T(1024)S(1)}, f32[1024]{0:T(1024)S(1)}) all-reduce(f32[6144]{0:T(1024)S(1)} %reduce_sum.194, f32[3072]{0:T(1024)S(1)} %convert_reduce_fusion.1, f32[1024]{0:T(1024)S(1)} %copy-done.64, ...), channel_id=5, replica_groups=mesh['blk'=8,'uly'=4] {'blk','uly'}, use_global_device_ids=true, to_apply=%region_26.27.clone | all-reduce | flops 15360 | bytes 122880
  921.5 153.3 %reduce-scatter.14.cloned.1.call-done = f32[32,3072]{1,0:T(8,128)} async-done(((f32[1024,3072]{1,0:T(8,128)}), f32[32,3072]{1,0:T(8,128)}) %reduce-scatter.14.cloned.1.call-update) | async-done | bytes 393232 | tf_op jit(solution)/shard_map/reduce_scatter | solution.py:311
  1074.9 185.0 %reduce-scatter.20.cloned.1.call-done = f32[128,1024]{1,0:T(8,128)} async-done(((f32[4096,1024]{1,0:T(8,128)}), f32[128,1024]{1,0:T(8,128)}) %reduce-scatter.20.cloned.1.call-update) | async-done | bytes 524304 | tf_op jit(solution)/shard_map/reduce_scatter | solution.py:317
  1259.9 187.3 %reduce-scatter.18.cloned.1.call-done = f32[32,4096]{1,0:T(8,128)} async-done(((f32[1024,4096]{1,0:T(8,128)}), f32[32,4096]{1,0:T(8,128)}) %reduce-scatter.18.cloned.1.call-update) | async-done | bytes 524304 | tf_op jit(solution)/shard_map/reduce_scatter | solution.py:315
  1447.1 255.4 %reduce-scatter.12.cloned.1.call-done = f32[32,6144]{1,0:T(8,128)} async-done(((f32[1024,6144]{1,0:T(8,128)}), f32[32,6144]{1,0:T(8,128)}) %reduce-scatter.12.cloned.1.call-update) | async-done | bytes 786448 | tf_op jit(solution)/shard_map/reduce_scatter | solution.py:309
  (499 shorter events, 312.0 us)
Async XLA Ops:
  7.2 368.4 %copy-start = (bf16[1024,1024]{1,0:T(8,128)(2,1)S(1)}, bf16[1024,1024]{1,0:T(8,128)(2,1)}, u32[]{:S(2)}) copy-start(bf16[1024,1024]{1,0:T(8,128)(2,1)} %param.30) | copy-start | bytes 6291460
  7.2 112.1 %all-gather.5.cloned.1.call-start = ((), (), s32[]{:S(2)}) async-start(), calls=%async_computation.16 | async-start | bytes 3686400 | tf_op jit(solution)/shard_map/all_gather | solution.py:123
  7.3 29.8 %copy-start.71 = (f32[32]{0:T(128)}, f32[32]{0:T(128)S(1)}, u32[]{:S(2)}) copy-start(f32[32]{0:T(128)S(1)} %fusion.78) | copy-start | bytes 388
  7.3 29.7 %copy-start.73 = (pred[32]{0:T(512)(128)(4,1)}, pred[32]{0:T(512)(128)(4,1)S(1)}, u32[]{:S(2)}) copy-start(pred[32]{0:T(512)(128)(4,1)S(1)} %get-tuple-element.561) | copy-start | bytes 100
  7.3 29.7 %copy-start.75 = (pred[32]{0:T(512)(128)(4,1)}, pred[32]{0:T(512)(128)(4,1)S(1)}, u32[]{:S(2)}) copy-start(pred[32]{0:T(512)(128)(4,1)S(1)} %get-tuple-element.562) | copy-start | bytes 100
  9.7 13.0 copy-start.58
  11.0 11.7 copy-start.61
  56.4 19.2 %copy-start.79 = (s32[64]{0:T(128)S(1)}, s32[64]{0:T(128)}, u32[]{:S(2)}) copy-start(s32[64]{0:T(128)} %param.25) | copy-start | bytes 772
  56.4 19.3 %copy-start.78 = (s32[64]{0:T(128)S(1)}, s32[64]{0:T(128)}, u32[]{:S(2)}) copy-start(s32[64]{0:T(128)} %param.24) | copy-start | bytes 772
  60.4 11.1 all-to-all-start.2
  71.4 11.8 all-to-all-start
  75.5 176.8 %all-gather.3.cloned.1.call-start = ((), (), s32[]{:S(2)}) async-start(), calls=%async_computation.15 | async-start | bytes 3686400 | tf_op jit(solution)/shard_map/all_gather | solution.py:124
  157.0 10.5 copy-start.42
  157.0 11.1 copy-start.45
  185.1 10.4 copy-start.42
  185.2 11.0 copy-start.45
  213.2 10.4 copy-start.42
  213.2 11.0 copy-start.45
  241.3 10.4 copy-start.42
  241.3 11.0 copy-start.45
  262.7 11.6 copy-start.46
  344.5 18.7 %copy-start.4 = (f32[800,4,64]{0,2,1:T(8,128)}, f32[800,4,64]{0,2,1:T(8,128)S(1)}, u32[]{:S(2)}) copy-start(f32[800,4,64]{0,2,1:T(8,128)S(1)} %get-tuple-element.195) | copy-start | bytes 2457604
  344.5 13.8 copy-start.54
  349.1 16.3 copy-start.47
  351.2 23.2 %all-to-all-start.3 = ((bf16[4,200,256]{2,1,0:T(8,128)(2,1)}), bf16[4,200,256]{2,1,0:T(8,128)(2,1)}, u32[]{:S(2)}, u32[]{:S(2)}) async-start(bf16[4,200,256]{2,1,0:T(8,128)(2,1)} %copy.85), calls=%async_computation.3 | async-start | bytes 819200 | tf_op jit(solution)/shard_map/all_to_all | solution.py:180
  359.4 9.3 copy-start.49
  378.5 19.4 %copy-start.7 = (f32[200,1024]{1,0:T(8,128)}, f32[200,1024]{1,0:T(8,128)S(1)}, u32[]{:S(2)}) copy-start(f32[200,1024]{1,0:T(8,128)S(1)} %get-tuple-element.520) | copy-start | bytes 2457604
  378.5 19.4 %copy-start.52 = (f32[200]{0:T(256)}, f32[200]{0:T(256)S(1)}, u32[]{:S(2)}) copy-start(f32[200]{0:T(256)S(1)} %broadcast_multiply_fusion.4) | copy-start | bytes 2404
  378.7 19.1 %copy-start.56 = (f32[200]{0:T(256)}, f32[200]{0:T(256)S(1)}, u32[]{:S(2)}) copy-start(f32[200]{0:T(256)S(1)} %add_rsqrt_fusion) | copy-start | bytes 2404
  379.0 14.9 slice-start
  384.5 9.4 copy-start.9
  384.5 9.4 slice-start.1
  400.5 13.8 copy-start.66
  401.3 11.1 all-to-all-start.4
  404.7 289.8 %reduce-scatter.24.cloned.1.call-start = ((), (), s32[]{:S(2)}) async-start(), calls=%async_computation.23 | async-start | bytes 3686400 | tf_op jit(solution)/shard_map/reduce_scatter | solution.py:261
  620.3 153.3 %reduce-scatter.22.cloned.1.call-start = ((), (), s32[]{:S(2)}) async-start(), calls=%async_computation.22 | async-start | bytes 3686400
  641.2 280.3 %reduce-scatter.16.cloned.1.call-start = ((), (), s32[]{:S(2)}) async-start(), calls=%async_computation.19 | async-start | bytes 4325376 | tf_op jit(solution)/shard_map/reduce_scatter | solution.py:313
  694.6 85.9 %all-to-all-start.7 = ((bf16[4,200,256]{2,1,0:T(8,128)(2,1)}), bf16[4,200,256]{2,1,0:T(8,128)(2,1)S(1)}, u32[]{:S(2)}, u32[]{:S(2)}) async-start(bf16[4,200,256]{2,1,0:T(8,128)(2,1)} %bitcast.231), calls=%async_computation.7 | async-start | bytes 819200 | tf_op jit(solution)/shard_map/all_to_all | solution.py:273
  780.4 12.8 all-to-all-start.6
  785.5 22.9 %copy-start.39 = (bf16[200,1024]{1,0:T(8,128)(2,1)S(1)}, bf16[200,1024]{1,0:T(8,128)(2,1)}, u32[]{:S(2)}) copy-start(bf16[200,1024]{1,0:T(8,128)(2,1)} %copy-done.38) | copy-start | bytes 1228804
  793.2 14.0 all-to-all-start.5
  796.7 278.1 %reduce-scatter.14.cloned.1.call-start = ((), (), s32[]{:S(2)}) async-start(), calls=%async_computation.18 | async-start | bytes 12976128 | tf_op jit(solution)/shard_map/reduce_scatter | solution.py:311
  814.8 445.1 %reduce-scatter.20.cloned.1.call-start = ((), (), s32[]{:S(2)}) async-start(), calls=%async_computation.21 | async-start | bytes 17301504 | tf_op jit(solution)/shard_map/reduce_scatter | solution.py:317
  826.0 621.1 %reduce-scatter.18.cloned.1.call-start = ((), (), s32[]{:S(2)}) async-start(), calls=%async_computation.20 | async-start | bytes 17301504 | tf_op jit(solution)/shard_map/reduce_scatter | solution.py:315
  835.8 866.8 %reduce-scatter.12.cloned.1.call-start = ((), (), s32[]{:S(2)}) async-start(), calls=%async_computation.17 | async-start | bytes 25952256 | tf_op jit(solution)/shard_map/reduce_scatter | solution.py:309
  848.3 12.0 copy-start.48
  848.3 11.9 copy-start.50
  876.8 825.8 %copy-start.1 = (bf16[1024,1024]{1,0:T(8,128)(2,1)S(1)}, bf16[1024,1024]{1,0:T(8,128)(2,1)}, u32[]{:S(2)}) copy-start(bf16[1024,1024]{1,0:T(8,128)(2,1)} %param.30) | copy-start | bytes 6291460
  (78 other events, 285.0 us)
Sparse Core Ops, SparseCore 0:
  56.5 62.7 all-gather.4
  121.4 60.4 all-gather.2
  620.4 74.0 reduce-scatter.23
  698.4 75.1 reduce-scatter.21
  776.3 140.2 reduce-scatter.15
  923.0 151.7 reduce-scatter.13
  1077.8 182.0 reduce-scatter.19
  1262.9 184.2 reduce-scatter.17
  1455.3 247.2 reduce-scatter.11
where the time goes:
time: 1720 us; the launch traced here: 1710 us
  waiting for transfers between devices  974 us (57%)
  matrix products  376 us (22%)
  local copies, waits for them, and re-layouts  170 us (10%)
  other arithmetic  93.1 us (5%)
  blocking collectives  53 us (3%)
  starting transfers between devices  26.5 us (2%)
    reduce_scatter x1, waiting for transfers between devices, on_device(): lax.psum_scatter(g_mod_weight, ('blk', 'uly'), scatter_dimension=0, tiled...  255 us
    reduce_scatter x1, waiting for transfers between devices, on_device(): lax.psum_scatter(g_up_weight, ('blk', 'uly'), scatter_dimension=0, tiled=...  187 us
    reduce_scatter x1, waiting for transfers between devices, on_device(): lax.psum_scatter(g_down_weight, ('blk', 'uly'), scatter_dimension=0, tile...  185 us
    reduce_scatter x1, waiting for transfers between devices, on_device(): lax.psum_scatter(g_attn_weight, ('blk', 'uly'), scatter_dimension=0, tile...  153 us
    dot_general x12, matrix products, piece_score(): jnp.einsum('qhd,khd->hqk', queries, k_rows, preferred_element_type=jnp.fl...  131 us
    unnamed x10, waiting for transfers between devices  75.7 us
    unnamed x175, local copies, waits for them, and re-layouts  73.7 us
    dot_general x4, matrix products, back_piece(): jnp.einsum('qhd,khd->hqk', attn_grad, v_rows, preferred_element_type=jnp....  50 us
  transfers between devices with their start and end apart: 16, of which 12 were waited for; matrix products, arithmetic and copies ran while one was open for 15% of the time, Pallas kernels for 0%

commit v1 on v0

--- a/solution.py
+++ b/solution.py
@@ -11,6 +11,22 @@
 GELU_C = 0.7978845608028654
 GELU_K = 0.044715
 NEG_BIG = -1e30
+
+
+def gather_around(x, axis, dim):
+    ways, here, lap = (lax.axis_size(axis), lax.axis_index(axis), x.shape[dim])
+    shape = [n * ways if d == dim else n for d, n in enumerate(x.shape)]
+    full = lax.dynamic_update_slice_in_dim(jnp.zeros(shape, x.dtype), x, here * lap, axis=dim)
+    going_up = going_down = x
+    for far in range(1, ways // 2 + 1):
+        going_up = lax.ppermute(going_up, axis, [(d, (d + 1) % ways) for d in range(ways)])
+        full = lax.dynamic_update_slice_in_dim(full, going_up, (here - far) % ways * lap, axis=dim)
+        if 2 * far < ways:
+            going_down = lax.ppermute(going_down, axis, [(d, (d - 1) % ways) for d in range(ways)])
+            full = lax.dynamic_update_slice_in_dim(
+                full, going_down, (here + far) % ways * lap, axis=dim
+            )
+    return full
 
 
 def layer_norm(values):
@@ -120,7 +136,7 @@
         lax.all_to_all(v_tok, "uly", split_axis=1, concat_axis=0, tiled=True),
     )
     k_every, v_every = (
-        lax.all_gather(k_heads, "blk", axis=0, tiled=True),
+        gather_around(k_heads, "blk", 0),
         lax.all_gather(v_heads, "blk", axis=0, tiled=True),
     )
     group = 2

time: 1720 us -> 1820 us (1.058)
  matrix products: 376 us -> 427 us
  local copies, waits for them, and re-layouts: 170 us -> 214 us
    dynamic_update_slice x0 -> x8, local copies, waits for them, and re-layouts: none -> 46.2 us  [the longest x4 22.7 us: gather_around(): lax.dynamic_update_slice_in_dim(full, going_up, (here - far) % ways * lap...]
    all_gather x1 -> x0, waiting for transfers between devices: 36 us -> none  [on_device(): lax.all_gather(k_heads, 'blk', axis=0, tiled=True)]
    ppermute x0 -> x7, waiting for transfers between devices: none -> 29 us  [the longest x4 28.9 us: gather_around(): lax.ppermute(going_up, axis, [(d, (d + 1) % ways) for d in range(ways)])]
    unnamed x10 -> x9, waiting for transfers between devices: 75.7 us -> 49.7 us
    dot_general x4, matrix products: 13.3 us -> 34.8 us  [mix_values(): jnp.einsum('hqk,khd->qhd', prob, v_rows.astype(jnp.float32), preferred_el...]
    unnamed x175 -> x183, local copies, waits for them, and re-layouts: 73.7 us -> 67.4 us
  transfers between devices with their start and end apart: 16 -> 22, of which waited for: 12 -> 15; matrix products, arithmetic and copies ran while one was open for 15% -> 17% of each run, Pallas kernels for 0% -> 0%
where the time goes in v1:
time: 1820 us; the launch traced here: 1800 us
  waiting for transfers between devices  963 us (53%)
  matrix products  427 us (23%)
  local copies, waits for them, and re-layouts  214 us (12%)
  other arithmetic  87.3 us (5%)
  blocking collectives  51.5 us (3%)
  starting transfers between devices  42.5 us (2%)
    reduce_scatter x1, waiting for transfers between devices, on_device(): lax.psum_scatter(g_mod_weight, ('blk', 'uly'), scatter_dimension=0, tiled...  255 us
    reduce_scatter x1, waiting for transfers between devices, on_device(): lax.psum_scatter(g_down_weight, ('blk', 'uly'), scatter_dimension=0, tile...  187 us
    reduce_scatter x1, waiting for transfers between devices, on_device(): lax.psum_scatter(g_up_weight, ('blk', 'uly'), scatter_dimension=0, tiled=...  185 us
    reduce_scatter x1, waiting for transfers between devices, on_device(): lax.psum_scatter(g_attn_weight, ('blk', 'uly'), scatter_dimension=0, tile...  158 us
    dot_general x12, matrix products, piece_score(): jnp.einsum('qhd,khd->hqk', queries, k_rows, preferred_element_type=jnp.fl...  141 us
    unnamed x183, local copies, waits for them, and re-layouts  67.4 us
    reduce_scatter x1, waiting for transfers between devices, on_device(): lax.psum_scatter(value_terms.astype(jnp.bfloat16), 'blk', scatter_dimensi...  57.7 us
    dot_general x4, matrix products, back_piece(): jnp.einsum('qhd,khd->hqk', attn_grad, v_rows, preferred_element_type=jnp....  50 us
  transfers between devices with their start and end apart: 22, of which 15 were waited for; matrix products, arithmetic and copies ran while one was open for 17% of the time, Pallas kernels for 0%

profile of v1, /device:TPU:0, one launch (start us, length us, event | category | flops | bytes accessed | tf_op | source)
XLA Modules:
  0.0 1803.3 jit_solution(15143291625145347449)
XLA Ops:
  45.5 11.6 all_to_all.131
  61.8 14.5 collective-permute-done
  81.9 13.7 collective-permute-done.2
  194.4 100.5 %while.41 = (s32[]{:T(128)}, f32[4,800]{1,0:T(4,128)S(1)}, f32[4,800]{1,0:T(4,128)S(1)}, s32[4,1600]{1,0:T(4,128)S(1)}, s32[4,1600]{1,0:T(4,128)S(1)}, /*index=5...) while((s32[]{:T(128)}, f32[4,800]{1,0:T(4,128)S(1)}, ...), condition=%wide.region_5.6_spmd.clone, body=%wide.region_2.5_spmd.clone.sunk | while | flops 700176000 | bytes 46341816 | solution.py:173
  196.5 13.0 fusion.152
  209.4 10.3 select_reduce_fusion.2
  221.5 12.9 fusion.152
  234.4 10.3 select_reduce_fusion.2
  246.5 12.9 fusion.152
  259.5 10.3 select_reduce_fusion.2
  271.5 12.9 fusion.152
  284.5 10.3 select_reduce_fusion.2
  295.5 10.3 reshape.864
  305.8 10.4 copy.104
  316.2 114.2 %while.42 = (s32[]{:T(128)}, f32[800,4,64]{0,2,1:T(8,128)S(1)}, f32[800,4,64]{0,2,1:T(8,128)}, bf16[4,1600,4,64]{1,3,2,0:T(8,128)(2,1)}, s32[4,1600]{1,0:T(4,128...) while((s32[]{:T(128)}, f32[800,4,64]{0,2,1:T(8,128)S(1)}, ...), condition=%wide.region_7.8_spmd.clone, body=%wide.region_6.7_spmd.clone.sunk | while | flops 1991219200 | bytes 81070936 | solution.py:192
  321.1 10.5 fusion.160
  349.5 10.5 fusion.160
  378.1 10.5 fusion.160
  388.6 8.7 fusion.162
  406.6 10.5 fusion.160
  462.4 9.4 convert_reduce_fusion
  492.1 200.4 %while.43 = (s32[]{:T(128)}, f32[800,4,64]{0,2,1:T(8,128)S(1)}, bf16[4,1600,4,64]{1,3,2,0:T(8,128)(2,1)}, bf16[4,1600,4,64]{1,3,2,0:T(8,128)(2,1)}, bf16[4,1600,...) while((s32[]{:T(128)}, f32[800,4,64]{0,2,1:T(8,128)S(1)}, ...), condition=%wide.region_13.14_spmd.clone, body=%wide.region_12.13_spmd.clone.sunk | while | flops 3322624000 | bytes 106510560 | solution.py:268
  494.2 11.7 fusion.173
  506.0 12.5 fusion.174
  532.8 9.7 fusion.177
  544.2 11.7 fusion.173
  556.0 12.5 fusion.174
  582.8 9.7 fusion.177
  594.2 11.7 fusion.173
  606.0 12.5 fusion.174
  632.8 9.7 fusion.177
  644.2 11.7 fusion.173
  656.0 12.5 fusion.174
  682.8 9.7 fusion.177
  692.5 10.5 copy.133
  703.0 10.4 reshape.860
  713.4 10.5 copy.134
  723.9 10.2 reshape.862
  739.5 49.5 %reduce-scatter.22.cloned.1.call-done = bf16[800,256]{1,0:T(8,128)(2,1)} async-done(((bf16[6400,256]{1,0:T(8,128)(2,1)}), bf16[800,256]{1,0:T(8,128)(2,1)}) %reduce-scatter.22.cloned.1.call-update) | async-done | bytes 409616
  810.4 57.7 %reduce-scatter.24.cloned.1.call-done = bf16[800,256]{1,0:T(8,128)(2,1)} async-done(((bf16[6400,256]{1,0:T(8,128)(2,1)}), bf16[800,256]{1,0:T(8,128)(2,1)}) %reduce-scatter.24.cloned.1.call-update) | async-done | bytes 409616 | tf_op jit(solution)/shard_map/reduce_scatter | solution.py:277
  898.8 10.2 fusion.82
  937.8 13.4 fusion.79
  951.9 39.9 %all-reduce.5 = (f32[6144]{0:T(1024)S(1)}, f32[3072]{0:T(1024)S(1)}, f32[1024]{0:T(1024)S(1)}, f32[4096]{0:T(1024)S(1)}, f32[1024]{0:T(1024)S(1)}) all-reduce(f32[6144]{0:T(1024)S(1)} %reduce_sum.194, f32[3072]{0:T(1024)S(1)} %convert_reduce_fusion.1, f32[1024]{0:T(1024)S(1)} %copy-done.63, ...), channel_id=5, replica_groups=mesh['blk'=8,'uly'=4] {'blk','uly'}, use_global_device_ids=true, to_apply=%region_26.27.clone | all-reduce | flops 15360 | bytes 122880
  994.8 15.9 reduce-scatter.16.cloned.1.call-done
  1010.7 157.8 %reduce-scatter.14.cloned.1.call-done = f32[32,3072]{1,0:T(8,128)} async-done(((f32[1024,3072]{1,0:T(8,128)}), f32[32,3072]{1,0:T(8,128)}) %reduce-scatter.14.cloned.1.call-update) | async-done | bytes 393232 | tf_op jit(solution)/shard_map/reduce_scatter | solution.py:327
  1168.5 184.7 %reduce-scatter.18.cloned.1.call-done = f32[32,4096]{1,0:T(8,128)} async-done(((f32[1024,4096]{1,0:T(8,128)}), f32[32,4096]{1,0:T(8,128)}) %reduce-scatter.18.cloned.1.call-update) | async-done | bytes 524304 | tf_op jit(solution)/shard_map/reduce_scatter | solution.py:331
  1353.3 187.5 %reduce-scatter.20.cloned.1.call-done = f32[128,1024]{1,0:T(8,128)} async-done(((f32[4096,1024]{1,0:T(8,128)}), f32[128,1024]{1,0:T(8,128)}) %reduce-scatter.20.cloned.1.call-update) | async-done | bytes 524304 | tf_op jit(solution)/shard_map/reduce_scatter | solution.py:333
  1540.8 255.3 %reduce-scatter.12.cloned.1.call-done = f32[32,6144]{1,0:T(8,128)} async-done(((f32[1024,6144]{1,0:T(8,128)}), f32[32,6144]{1,0:T(8,128)}) %reduce-scatter.12.cloned.1.call-update) | async-done | bytes 786448 | tf_op jit(solution)/shard_map/reduce_scatter | solution.py:325
  (511 shorter events, 422.4 us)
Async XLA Ops:
  7.2 446.3 %copy-start = (bf16[1024,1024]{1,0:T(8,128)(2,1)S(1)}, bf16[1024,1024]{1,0:T(8,128)(2,1)}, u32[]{:S(2)}) copy-start(bf16[1024,1024]{1,0:T(8,128)(2,1)} %param.30) | copy-start | bytes 6291460
  7.2 31.0 %copy-start.72 = (pred[32]{0:T(512)(128)(4,1)}, pred[32]{0:T(512)(128)(4,1)S(1)}, u32[]{:S(2)}) copy-start(pred[32]{0:T(512)(128)(4,1)S(1)} %get-tuple-element.561) | copy-start | bytes 100
  7.2 31.0 %copy-start.74 = (pred[32]{0:T(512)(128)(4,1)}, pred[32]{0:T(512)(128)(4,1)S(1)}, u32[]{:S(2)}) copy-start(pred[32]{0:T(512)(128)(4,1)S(1)} %get-tuple-element.562) | copy-start | bytes 100
  7.3 30.9 %copy-start.76 = (f32[32]{0:T(128)}, f32[32]{0:T(128)S(1)}, u32[]{:S(2)}) copy-start(f32[32]{0:T(128)S(1)} %fusion.78) | copy-start | bytes 388
  9.7 14.5 copy-start.58
  10.9 13.2 copy-start.60
  57.1 41.3 %copy-start.38 = (bf16[200,4,256]{2,0,1:T(8,128)(2,1)}, bf16[200,4,256]{2,0,1:T(8,128)(2,1)S(1)}, u32[]{:S(2)}) copy-start(bf16[200,4,256]{2,0,1:T(8,128)(2,1)S(1)} %all_to_all.131) | copy-start | bytes 1228804
  57.1 19.2 %collective-permute-start = (bf16[800,256]{1,0:T(8,128)(2,1)S(1)}, bf16[800,256]{1,0:T(8,128)(2,1)S(1)}, u32[]{:S(2)}, u32[]{:S(2)}) collective-permute-start(bf16[800,256]{1,0:T(8,128)(2,1)S(1)} %bitcast.224), channel_id=1, source_target_pairs={{0,4},{4,8},{8,12},{12,16},{16,20},{20,24},{24,28},{28,0},{1,5},{5... | collective-permute-start | bytes 1228808 | tf_op jit(solution)/shard_map/ppermute | solution.py:22
  58.6 20.2 %collective-permute-start.1 = (bf16[800,256]{1,0:T(8,128)(2,1)S(1)}, bf16[800,256]{1,0:T(8,128)(2,1)S(1)}, u32[]{:S(2)}, u32[]{:S(2)}) collective-permute-start(bf16[800,256]{1,0:T(8,128)(2,1)S(1)} %bitcast.225), channel_id=1, source_target_pairs={{0,28},{4,0},{8,4},{12,8},{16,12},{20,16},{24,20},{28,24},{1,29},{... | collective-permute-start | bytes 1228808 | tf_op jit(solution)/shard_map/ppermute | solution.py:25
  76.3 22.1 %copy-start.42 = (bf16[800,256]{1,0:T(8,128)(2,1)}, bf16[800,256]{1,0:T(8,128)(2,1)S(1)}, u32[]{:S(2)}) copy-start(bf16[800,256]{1,0:T(8,128)(2,1)S(1)} %collective-permute-done) | copy-start | bytes 1228804
  76.3 19.3 %collective-permute-start.2 = (bf16[800,256]{1,0:T(8,128)(2,1)S(1)}, bf16[800,256]{1,0:T(8,128)(2,1)}, u32[]{:S(2)}, u32[]{:S(2)}) collective-permute-start(bf16[800,256]{1,0:T(8,128)(2,1)S(1)} %collective-permute-done), channel_id=1, source_target_pairs={{0,4},{4,8},{8,12},{12,16},{16,20},{20,24},{24,28},{28,0},{1,5},{5... | collective-permute-start | bytes 1228808 | tf_op jit(solution)/shard_map/ppermute | solution.py:22
  78.8 34.7 %copy-start.41 = (bf16[800,256]{1,0:T(8,128)(2,1)}, bf16[800,256]{1,0:T(8,128)(2,1)S(1)}, u32[]{:S(2)}) copy-start(bf16[800,256]{1,0:T(8,128)(2,1)S(1)} %collective-permute-done.1) | copy-start | bytes 1228804
  78.8 27.1 %collective-permute-start.3 = (bf16[800,256]{1,0:T(8,128)(2,1)S(1)}, bf16[800,256]{1,0:T(8,128)(2,1)}, u32[]{:S(2)}, u32[]{:S(2)}) collective-permute-start(bf16[800,256]{1,0:T(8,128)(2,1)S(1)} %collective-permute-done.1), channel_id=1, source_target_pairs={{0,28},{4,0},{8,4},{12,8},{16,12},{20,16},{24,20},{28,24},{1,29},{... | collective-permute-start | bytes 1228808 | tf_op jit(solution)/shard_map/ppermute | solution.py:25
  95.6 14.1 collective-permute-start.4
  101.4 16.3 copy-start.80
  101.4 16.4 copy-start.79
  102.4 11.1 all-to-all-start.2
  105.9 62.4 %collective-permute-start.5 = (bf16[800,256]{1,0:T(8,128)(2,1)}, bf16[800,256]{1,0:T(8,128)(2,1)}, u32[]{:S(2)}, u32[]{:S(2)}) collective-permute-start(bf16[800,256]{1,0:T(8,128)(2,1)} %collective-permute-done.3), channel_id=1, source_target_pairs={{0,28},{4,0},{8,4},{12,8},{16,12},{20,16},{24,20},{28,24},{1,29},{... | collective-permute-start | bytes 1228808 | tf_op jit(solution)/shard_map/ppermute | solution.py:25
  109.7 65.8 %collective-permute-start.6 = (bf16[800,256]{1,0:T(8,128)(2,1)}, bf16[800,256]{1,0:T(8,128)(2,1)}, u32[]{:S(2)}, u32[]{:S(2)}) collective-permute-start(bf16[800,256]{1,0:T(8,128)(2,1)} %collective-permute-done.4), channel_id=1, source_target_pairs={{0,4},{4,8},{8,12},{12,16},{16,20},{20,24},{24,28},{28,0},{1,5},{5... | collective-permute-start | bytes 1228808 | tf_op jit(solution)/shard_map/ppermute | solution.py:22
  113.5 11.8 all-to-all-start
  117.6 177.9 %all-gather.2.cloned.1.call-start = ((), (), s32[]{:S(2)}) async-start(), calls=%async_computation.15 | async-start | bytes 3686400 | tf_op jit(solution)/shard_map/all_gather | solution.py:140
  305.8 10.4 copy-start.3
  305.8 10.4 copy-start.6
  430.5 9.5 copy-start.47
  432.8 10.4 copy-start.54
  433.9 18.4 %all-to-all-start.3 = ((bf16[4,200,256]{2,1,0:T(8,128)(2,1)}), bf16[4,200,256]{2,1,0:T(8,128)(2,1)}, u32[]{:S(2)}, u32[]{:S(2)}) async-start(bf16[4,200,256]{2,1,0:T(8,128)(2,1)} %copy.106), calls=%async_computation.3 | async-start | bytes 819200 | tf_op jit(solution)/shard_map/all_to_all | solution.py:196
  456.3 19.4 %copy-start.4 = (f32[200,1024]{1,0:T(8,128)}, f32[200,1024]{1,0:T(8,128)S(1)}, u32[]{:S(2)}) copy-start(f32[200,1024]{1,0:T(8,128)S(1)} %get-tuple-element.520) | copy-start | bytes 2457604
  456.3 19.4 %copy-start.51 = (f32[200]{0:T(256)}, f32[200]{0:T(256)S(1)}, u32[]{:S(2)}) copy-start(f32[200]{0:T(256)S(1)} %broadcast_multiply_fusion.4) | copy-start | bytes 2404
  456.6 19.1 %copy-start.56 = (f32[200]{0:T(256)}, f32[200]{0:T(256)S(1)}, u32[]{:S(2)}) copy-start(f32[200]{0:T(256)S(1)} %add_rsqrt_fusion) | copy-start | bytes 2404
  456.9 14.9 slice-start
  462.3 9.4 copy-start.7
  462.4 9.4 slice-start.1
  478.3 13.8 copy-start.65
  479.1 11.1 all-to-all-start.4
  482.6 306.5 %reduce-scatter.22.cloned.1.call-start = ((), (), s32[]{:S(2)}) async-start(), calls=%async_computation.21 | async-start | bytes 3686400
  713.4 154.7 %reduce-scatter.24.cloned.1.call-start = ((), (), s32[]{:S(2)}) async-start(), calls=%async_computation.22 | async-start | bytes 3686400 | tf_op jit(solution)/shard_map/reduce_scatter | solution.py:277
  734.2 276.5 %reduce-scatter.16.cloned.1.call-start = ((), (), s32[]{:S(2)}) async-start(), calls=%async_computation.18 | async-start | bytes 4325376 | tf_op jit(solution)/shard_map/reduce_scatter | solution.py:329
  795.8 11.1 all-to-all-start.6
  802.0 79.8 %copy-start.36 = (bf16[200,1024]{1,0:T(8,128)(2,1)S(1)}, bf16[200,1024]{1,0:T(8,128)(2,1)}, u32[]{:S(2)}) copy-start(bf16[200,1024]{1,0:T(8,128)(2,1)} %copy-done.35) | copy-start | bytes 1228804
  806.9 61.2 %all-to-all-start.5 = ((bf16[4,200,256]{2,1,0:T(8,128)(2,1)}), bf16[4,200,256]{2,1,0:T(8,128)(2,1)S(1)}, u32[]{:S(2)}, u32[]{:S(2)}) async-start(bf16[4,200,256]{2,1,0:T(8,128)(2,1)} %copy.112), calls=%async_computation.5 | async-start | bytes 819200 | tf_op jit(solution)/shard_map/all_to_all | solution.py:287
  868.1 12.5 all-to-all-start.7
  871.6 297.0 %reduce-scatter.14.cloned.1.call-start = ((), (), s32[]{:S(2)}) async-start(), calls=%async_computation.17 | async-start | bytes 12976128 | tf_op jit(solution)/shard_map/reduce_scatter | solution.py:327
  888.1 465.1 %reduce-scatter.18.cloned.1.call-start = ((), (), s32[]{:S(2)}) async-start(), calls=%async_computation.19 | async-start | bytes 17301504 | tf_op jit(solution)/shard_map/reduce_scatter | solution.py:331
  897.8 643.0 %reduce-scatter.20.cloned.1.call-start = ((), (), s32[]{:S(2)}) async-start(), calls=%async_computation.20 | async-start | bytes 17301504 | tf_op jit(solution)/shard_map/reduce_scatter | solution.py:333
  909.1 887.0 %reduce-scatter.12.cloned.1.call-start = ((), (), s32[]{:S(2)}) async-start(), calls=%async_computation.16 | async-start | bytes 25952256 | tf_op jit(solution)/shard_map/reduce_scatter | solution.py:325
  922.8 11.9 copy-start.48
  922.8 11.9 copy-start.50
  951.2 844.8 %copy-start.1 = (bf16[1024,1024]{1,0:T(8,128)(2,1)S(1)}, bf16[1024,1024]{1,0:T(8,128)(2,1)}, u32[]{:S(2)}) copy-start(bf16[1024,1024]{1,0:T(8,128)(2,1)} %param.30) | copy-start | bytes 6291460
  (76 other events, 303.3 us)
Sparse Core Ops, SparseCore 0:
  125.4 61.3 all-gather.1
  713.5 75.4 reduce-scatter.21
  793.0 75.0 reduce-scatter.23
  870.8 139.8 reduce-scatter.15
  1017.2 151.3 reduce-scatter.13
  1171.4 181.8 reduce-scatter.17
  1356.2 184.4 reduce-scatter.19
  1548.9 247.1 reduce-scatter.11
